TPU v7x, 32 devices: a whole 2x2x4 slice. The times are simulated.
32 devices in a mesh: inner: 4 (over y, x), outer: 8 (over z, core).
Axes of the slice: x: 2, y: 2, z: 4, core: 2. Of those that a mesh axis runs over, the one named last changes fastest.
Arguments:
- jac: float32 [512, 256, 256], P(('outer', 'inner')), may hold values from -0.5 to 1
- obs: float32 [512, 256], P(('outer', 'inner')), may hold values from -6 to 6
- gain_filter: float32 [256], replicated, may hold values from 0 to 0.1
- gain_smooth: float32 [256, 256], replicated, may hold values from -0.5 to 1
- init_mean: float32 [256], replicated, may hold values from -6 to 6
Outputs:
- filtered: float32 [512, 256], P(('outer', 'inner'))
- smoothed: float32 [512, 256], P(('outer', 'inner'))
All inputs are finite; a program needn't handle non-finite values.
Results may differ from a plain program's by a relative error of at most 0.0003.
Values sent between devices are 32-bit elements; how exact they have to be, the bound alone decides.
A program may use at most 64 MiB of HBM per device.

v0:
```python
import jax
import jax.numpy as jnp
from jax import lax
from jax.sharding import PartitionSpec as P

HIGHEST = lax.Precision.HIGHEST


def entering(part, axis, combine, identity):
    place = lax.axis_index(axis)
    gathered = lax.all_gather(part, axis)
    state = jnp.zeros_like(part) + jnp.asarray(identity, part.dtype)

    def one(turn, state):
        return combine(state, lax.dynamic_index_in_dim(gathered, turn, 0, False))

    return lax.fori_loop(0, place, one, state)


def last_row(state_width):
    return (jnp.arange(state_width + 1) == state_width).astype(jnp.float32)[:, None]


def identity_map(state_width):
    return jnp.concatenate(
        [jnp.eye(state_width, dtype=jnp.float32), jnp.zeros((1, state_width), jnp.float32)], 0
    )


def compose(earlier, later):
    state_width = later.shape[1]
    product = jnp.dot(earlier, later[:state_width], precision=HIGHEST)
    return product + last_row(state_width) * later[state_width][None, :]


def advance(packed, state):
    state_width = packed.shape[1]
    return jnp.dot(state, packed[:state_width], precision=HIGHEST) + packed[state_width]


def raise_power(factor, count):
    result = jnp.eye(factor.shape[0], dtype=jnp.float32)
    square = factor
    while count > 0:
        if count % 2 == 1:
            result = jnp.dot(result, square, precision=HIGHEST)
        count = count // 2
        if count > 0:
            square = jnp.dot(square, square, precision=HIGHEST)
    return result


def incoming_state(own_map, boundary):
    state_width = own_map.shape[1]
    identity = identity_map(state_width)
    inner_count = lax.axis_size("inner")
    inner_here = lax.axis_index("inner")
    gathered = lax.all_gather(own_map[None], "inner", axis=0, tiled=True)

    def absorb(running, inputs):
        before, group_total = running
        segment, position = inputs
        group_total = compose(group_total, segment)
        taken = position < inner_here
        before = jnp.where(taken, group_total, before)
        return ((before, group_total), None)

    (seg_before, group_total), _ = lax.scan(
        absorb,
        (identity, identity),
        (gathered, jnp.arange(inner_count, dtype=jnp.int32)),
        reverse=False,
    )
    group_before = entering(group_total, "outer", compose, identity)
    group_state = advance(group_before, boundary)
    return advance(seg_before, group_state)


def entering_backward(offset_sum, step_power):
    inner_count = lax.axis_size("inner")
    inner_here = lax.axis_index("inner")
    outer_count = lax.axis_size("outer")
    outer_here = lax.axis_index("outer")
    zero_state = jnp.zeros_like(offset_sum)
    seg_offsets = lax.all_gather(offset_sum[None], "inner", axis=0, tiled=True)

    def run_affine(power, here):

        def turn(running, inputs):
            state, caught = running
            offset, position = inputs
            caught = jnp.where(position == here, state, caught)
            state = jnp.dot(state, power, precision=HIGHEST) + offset
            return ((state, caught), None)

        return turn

    (group_offset, _), _ = lax.scan(
        run_affine(step_power, inner_here),
        (zero_state, zero_state),
        (seg_offsets, jnp.arange(inner_count, dtype=jnp.int32)),
        reverse=True,
    )
    group_power = raise_power(step_power, inner_count)
    group_offsets = lax.all_gather(group_offset[None], "outer", axis=0, tiled=True)
    (_, group_state), _ = lax.scan(
        run_affine(group_power, outer_here),
        (zero_state, zero_state),
        (group_offsets, jnp.arange(outer_count, dtype=jnp.int32)),
        reverse=True,
    )
    (_, device_state), _ = lax.scan(
        run_affine(step_power, inner_here),
        (group_state, group_state),
        (seg_offsets, jnp.arange(inner_count, dtype=jnp.int32)),
        reverse=True,
    )
    return device_state


def shards(jac, obs, gain_filter, gain_smooth, init_mean):
    state_width = jac.shape[1]
    step_count = jac.shape[0]
    retain = 1.0 - gain_filter
    bottom = last_row(state_width)

    def compose_forward(packed, inputs):
        step_matrix, measured = inputs
        moved = (
            lax.dot_general(packed, step_matrix, (((1,), (1,)), ((), ())), precision=HIGHEST)
            * retain[None, :]
        )
        return (moved + bottom * (gain_filter * measured)[None, :], None)

    forward_map, _ = lax.scan(compose_forward, identity_map(state_width), (jac, obs))
    start_state = incoming_state(forward_map, init_mean)

    def forward(state, inputs):
        step_matrix, measured = inputs
        predicted = jnp.dot(step_matrix, state, precision=HIGHEST)
        updated = predicted + gain_filter * (measured - predicted)
        return (updated, (predicted, updated))

    _, (predicted_all, filtered_all) = lax.scan(forward, start_state, (jac, obs))
    correction = filtered_all - predicted_all

    def backward(state, term):
        renewed = jnp.dot(gain_smooth, state, precision=HIGHEST) + term
        return (renewed, renewed)

    zero_state = jnp.zeros((state_width,), jnp.float32)
    offset_sum, _ = lax.scan(backward, zero_state, correction, reverse=True)
    step_power = raise_power(gain_smooth.T, step_count)
    after_state = entering_backward(offset_sum, step_power)
    _, back_states = lax.scan(backward, after_state, correction, reverse=True)
    return (filtered_all, predicted_all + back_states)


def solution(mesh):
    return jax.shard_map(
        shards,
        mesh=mesh,
        in_specs=(P(("outer", "inner"), None, None), P(("outer", "inner"), None), P(), P(), P()),
        out_specs=(P(("outer", "inner"), None), P(("outer", "inner"), None)),
        check_vma=False,
    )
```

profile of v0, /device:TPU:0, one launch (start us, length us, event | category | flops | bytes accessed | tf_op | source)
XLA Modules:
  0.0 221.8 jit_solution(6826046817942252627)
XLA Ops:
  8.0 34.7 %while.131 = (s32[]{:T(128)}, f32[257,256]{1,0:T(8,128)S(1)}, f32[16,256,256]{2,1,0:T(8,128)}, f32[256]{0:T(256)S(1)}, f32[256]{0:T(256)}, /*index=5*/f32[16,256]{1,0:T(8,128)}, s32[]{:T(128)}) while((s32[]{:T(128)}, f32[257,256]{1,0:T(8,128)S(1)}, f32[16,256,256]{2,1,0:T(8,128)}, f32[256]{0:T(256)S(1)}, f32[256]{0:T(256)}, ...), condition=%wide.region_1.2_spmd.clone, body=%wide.region_0.1_spmd.clone.sunk | while | flops 202311168 | bytes 1322585 | solution.py:135
  8.8 1.4 fusion.109
  10.9 1.4 fusion.109
  13.1 1.4 fusion.109
  15.3 1.4 fusion.109
  17.4 1.4 fusion.109
  19.6 1.4 fusion.109
  21.8 1.4 fusion.109
  23.9 1.4 fusion.109
  26.1 1.4 fusion.109
  28.3 1.4 fusion.109
  30.5 1.4 fusion.109
  32.6 1.4 fusion.109
  34.8 1.4 fusion.109
  37.0 1.4 fusion.109
  39.1 1.4 fusion.109
  41.3 1.4 fusion.109
  43.5 29.5 %all-gather.11.cloned.1.call-done = f32[4,257,256]{2,1,0:T(8,128)} async-done(((f32[1,257,256]{2,1,0:T(8,128)}), f32[4,257,256]{2,1,0:T(8,128)}) %all-gather.11.cloned.1.call-update) | async-done | bytes 1052688 | tf_op jit(solution)/shard_map/all_gather | solution.py:58
  73.1 14.0 %while.126 = (s32[]{:T(128)}, f32[257,256]{1,0:T(8,128)S(1)}, f32[257,256]{1,0:T(8,128)S(1)}, s32[4]{0:T(128)S(1)}, s32[]{:T(128)}, /*index=5*/f32[4,257,256]{2,1,0:T(8,128)}, s32[]{:T(128)}, s32[]{:T(128)}, s32[]{}) while((s32[]{:T(128)}, f32[257,256]{1,0:T(8,128)S(1)}, f32[257,256]{1,0:T(8,128)S(1)}, s32[4]{0:T(128)S(1)}, s32[]{:T(128)}, ...), condition=%wide.region_3.4_spmd, body=%wide.region_2.3_spmd.sunk | while | flops 202310912 | bytes 1846927 | solution.py:68
  75.1 1.5 broadcast_select_fusion.9
  78.6 1.5 broadcast_select_fusion.9
  82.1 1.5 broadcast_select_fusion.9
  85.6 1.5 broadcast_select_fusion.9
  91.0 26.7 %all-gather.13.cloned.1.call-done = f32[8,257,256]{2,1,0:T(8,128)} async-done(((f32[1,257,256]{2,1,0:T(8,128)}), f32[8,257,256]{2,1,0:T(8,128)}) %all-gather.13.cloned.1.call-update) | async-done | bytes 2105360 | tf_op jit(solution)/shard_map/all_gather | solution.py:11
  118.3 33.3 %while.128 = (s32[]{:T(128)}, f32[256]{0:T(256)S(1)}, f32[16,256]{1,0:T(8,128)S(1)}, f32[16,256]{1,0:T(8,128)S(1)}, f32[16,256,256]{2,1,0:T(8,128)}, /*index=5*/...) while((s32[]{:T(128)}, f32[256]{0:T(256)S(1)}, f32[16,256]{1,0:T(8,128)S(1)}, ...), condition=%wide.region_7.8_spmd, body=%wide.region_6.7_spmd.sunk | while | flops 787202 | bytes 275049 | solution.py:144
  124.6 1.2 fusion.99
  151.6 6.1 %while.132 = (s32[]{:T(128)}, f32[256]{0:T(256)S(1)}, f32[256,256]{1,0:T(8,128)S(1)}, f32[16,256]{1,0:T(8,128)S(1)}, s32[]{:T(128)}, /*index=5*/s32[]{:T(128)}, s32[]{:T(128)}) while((s32[]{:T(128)}, f32[256]{0:T(256)S(1)}, f32[256,256]{1,0:T(8,128)S(1)}, f32[16,256]{1,0:T(8,128)S(1)}, s32[]{:T(128)}, /*index=5*/s32[]{:T(128)}, ...), condition=%wide.region_9.10_spmd.clone, body=%wide.region_8.9_spmd.clone.sunk | while | flops 786948 | bytes 271463 | solution.py:152
  157.7 8.0 %all-gather.6 = f32[4,1,256]{2,1,0:T(1,128)S(1)} all-gather(f32[1,1,256]{2,1,0:T(1,128)S(1)} %bitcast.222), channel_id=4, replica_groups=mesh['inner'=4,'outer'=8] {'inner'}, dimensions={0}, use_global_device_ids=true | all-gather | bytes 5120 | tf_op jit(solution)/shard_map/all_gather | solution.py:85
  166.9 22.8 %all-gather.7 = f32[8,1,256]{2,1,0:T(1,128)S(1)} all-gather(f32[1,1,256]{2,1,0:T(1,128)S(1)} %bitcast.221), channel_id=5, replica_groups=mesh['inner'=4,'outer'=8] {'outer'}, dimensions={0}, use_global_device_ids=true | all-gather | bytes 9216 | tf_op jit(solution)/shard_map/all_gather | solution.py:105
  189.7 12.2 %while.134 = (s32[]{:T(128)}, f32[256]{0:T(256)S(1)}, f32[256]{0:T(256)S(1)}, f32[256,256]{1,0:T(8,128)S(1)}, f32[8,256]{1,0:T(8,128)S(1)}, /*index=5*/s32[8]{0:...) while((s32[]{:T(128)}, f32[256]{0:T(256)S(1)}, f32[256]{0:T(256)S(1)}, ...), condition=%wide.region_13.14_spmd.clone, body=%wide.region_12.13_spmd.clone.sunk | while | flops 787461 | bytes 273557 | solution.py:106
  201.9 6.0 %while.129 = (s32[]{:T(128)}, f32[256]{0:T(256)S(1)}, f32[256]{0:T(256)S(1)}, f32[256,256]{1,0:T(8,128)S(1)}, f32[4,256]{1,0:T(4,128)S(1)}, /*index=5*/s32[4]{0:T(128)S(1)}, s32[]{:T(128)}, s32[]{:T(128)}, s32[]{:T(128)}) while((s32[]{:T(128)}, f32[256]{0:T(256)S(1)}, f32[256]{0:T(256)S(1)}, f32[256,256]{1,0:T(8,128)S(1)}, ...), condition=%wide.region_15.16_spmd, body=%wide.region_14.15_spmd.sunk | while | flops 786948 | bytes 272515 | solution.py:112
  207.9 6.3 %while.130 = (s32[]{:T(128)}, f32[256]{0:T(256)S(1)}, f32[16,256]{1,0:T(8,128)S(1)}, f32[256,256]{1,0:T(8,128)S(1)}, f32[16,256]{1,0:T(8,128)S(1)}, /*index=5*/s32[]{:T(128)}, s32[]{:T(128)}, s32[]{:T(128)}) while((s32[]{:T(128)}, f32[256]{0:T(256)S(1)}, f32[16,256]{1,0:T(8,128)S(1)}, f32[256,256]{1,0:T(8,128)S(1)}, ...), condition=%wide.region_17.18_spmd, body=%wide.region_16.17_spmd.sunk | while | flops 786691 | bytes 271465 | solution.py:155
  (400 shorter events, 79.2 us)
Async XLA Ops:
  7.2 110.5 %copy-start = (f32[256]{0:T(256)S(1)}, f32[256]{0:T(256)}, u32[]{:S(2)}) copy-start(f32[256]{0:T(256)} %param.27) | copy-start | bytes 3076
  7.2 65.9 %all-gather.11.cloned.1.call-start = ((), (), s32[]{:S(2)}) async-start(), calls=%async_computation | async-start | bytes 1351680 | tf_op jit(solution)/shard_map/all_gather | solution.py:58
  42.7 0.7 copy-start.3
  43.4 74.2 %all-gather.13.cloned.1.call-start = ((), (), s32[]{:S(2)}) async-start(), calls=%async_computation.1 | async-start | bytes 2433024 | tf_op jit(solution)/shard_map/all_gather | solution.py:11
  73.1 14.8 %copy-start.1 = (f32[256,256]{1,0:T(8,128)S(1)}, f32[256,256]{1,0:T(8,128)}, u32[]{:S(2)}) copy-start(f32[256,256]{1,0:T(8,128)} %param.26) | copy-start | bytes 786436
  87.1 0.7 copy-start.2
  117.6 0.7 copy-start.4
  151.6 38.1 %copy-start.5 = (f32[16,256]{1,0:T(8,128)}, f32[16,256]{1,0:T(8,128)S(1)}, u32[]{:S(2)}) copy-start(f32[16,256]{1,0:T(8,128)S(1)} %get-tuple-element.684) | copy-start | bytes 49156
Sparse Core Ops, SparseCore 0:
  43.5 29.4 all-gather.10
  87.9 29.6 all-gather.12
where the time goes:
time: 225 us; the launch traced here: 222 us
  matrix products  62.5 us (28%)
  waiting for transfers between devices  56.2 us (25%)
  blocking collectives  30.9 us (14%)
  local copies, waits for them, and re-layouts  30.6 us (14%)
  between operations  14.4 us (6%)
  other arithmetic  14.1 us (6%)
  loops' own time  13 us (6%)
    all_gather x1, waiting for transfers between devices, incoming_state(): gathered = lax.all_gather(own_map[None], 'inner', axis=0, tiled=True)  29.5 us
    all_gather x1, waiting for transfers between devices, entering(): gathered = lax.all_gather(part, axis)  26.7 us
    all_gather x1, blocking collectives, entering_backward(): lax.all_gather(group_offset[None], 'outer', axis=0, tiled=True)  22.8 us
    dot_general x16, matrix products, compose_forward(): lax.dot_general(packed, step_matrix, (((1,), (1,)), ((), ())), precision=...  21.9 us
    dot_general x16, matrix products, forward(): predicted = jnp.dot(step_matrix, state, precision=HIGHEST)  19.5 us
    dynamic_slice x48, local copies, waits for them, and re-layouts, shards(): lax.scan(compose_forward, identity_map(state_width), (jac, obs))  13.3 us
    mul x16, other arithmetic, compose_forward(): return (moved + bottom * (gain_filter * measured)[None, :], None)  11.6 us
    dot_general x32, matrix products, backward(): renewed = jnp.dot(gain_smooth, state, precision=HIGHEST) + term  8.65 us
  transfers between devices with their start and end apart: 2, of which 2 were waited for; matrix products, arithmetic and copies ran while one was open for 1% of the time, Pallas kernels for 0%

commit v1 on v0

--- a/solution.py
+++ b/solution.py
@@ -55,7 +55,9 @@
     identity = identity_map(state_width)
     inner_count = lax.axis_size("inner")
     inner_here = lax.axis_index("inner")
-    gathered = lax.all_gather(own_map[None], "inner", axis=0, tiled=True)
+    gathered = jnp.concatenate(
+        lax.all_to_all(jnp.stack([own_map[None]] * lax.axis_size("inner")), "inner", 0, 0), axis=0
+    )
 
     def absorb(running, inputs):
         before, group_total = running

time: 225 us -> 209 us (0.929)
  waiting for transfers between devices: 56.2 us -> 40.6 us
  starting transfers between devices: 0.08 us -> 5.19 us
  matrix products: 62.5 us -> 58.8 us
    all_gather x1 -> x0, waiting for transfers between devices: 29.5 us -> none  [incoming_state(): gathered = lax.all_gather(own_map[None], 'inner', axis=0, tiled=True)]
    all_to_all x0 -> x1, waiting for transfers between devices: none -> 13.6 us  [incoming_state(): lax.all_to_all(jnp.stack([own_map[None]] * lax.axis_size('inner')), 'inne...]
    all_to_all x0 -> x1, starting transfers between devices: none -> 5.19 us  [incoming_state(): lax.all_to_all(jnp.stack([own_map[None]] * lax.axis_size('inner')), 'inne...]
    dot_general x4, matrix products: 5.96 us -> 2.19 us  [compose(): product = jnp.dot(earlier, later[:state_width], precision=HIGHEST)]
    slice x4, local copies, waits for them, and re-layouts: 2.85 us -> 0.04 us  [compose(): return product + last_row(state_width) * later[state_width][None, :]]
  transfers between devices with their start and end apart: 2 -> 2, of which waited for: 2 -> 2; matrix products, arithmetic and copies ran while one was open for 1% -> 2% of each run, Pallas kernels for 0% -> 0%
where the time goes in v1:
time: 209 us; the launch traced here: 206 us
  matrix products  58.8 us (28%)
  waiting for transfers between devices  40.6 us (19%)
  blocking collectives  30.9 us (15%)
  local copies, waits for them, and re-layouts  28.7 us (14%)
  between operations  14.4 us (7%)
  other arithmetic  14.1 us (7%)
  loops' own time  13.1 us (6%)
  starting transfers between devices  5.19 us (2%)
    all_gather x1, waiting for transfers between devices, entering(): gathered = lax.all_gather(part, axis)  27 us
    all_gather x1, blocking collectives, entering_backward(): lax.all_gather(group_offset[None], 'outer', axis=0, tiled=True)  22.8 us
    dot_general x16, matrix products, compose_forward(): lax.dot_general(packed, step_matrix, (((1,), (1,)), ((), ())), precision=...  21.9 us
    dot_general x16, matrix products, forward(): predicted = jnp.dot(step_matrix, state, precision=HIGHEST)  19.5 us
    all_to_all x1, waiting for transfers between devices, incoming_state(): lax.all_to_all(jnp.stack([own_map[None]] * lax.axis_size('inner')), 'inne...  13.6 us
    dynamic_slice x48, local copies, waits for them, and re-layouts, shards(): lax.scan(compose_forward, identity_map(state_width), (jac, obs))  13.3 us
    mul x16, other arithmetic, compose_forward(): return (moved + bottom * (gain_filter * measured)[None, :], None)  11.6 us
    dot_general x32, matrix products, backward(): renewed = jnp.dot(gain_smooth, state, precision=HIGHEST) + term  8.65 us
  transfers between devices with their start and end apart: 2, of which 2 were waited for; matrix products, arithmetic and copies ran while one was open for 2% of the time, Pallas kernels for 0%

profile of v1, /device:TPU:0, one launch (start us, length us, event | category | flops | bytes accessed | tf_op | source)
XLA Modules:
  0.0 205.7 jit_solution(2330421047805529331)
XLA Ops:
  8.0 34.7 %while.131 = (s32[]{:T(128)}, f32[257,256]{1,0:T(8,128)S(1)}, f32[16,256,256]{2,1,0:T(8,128)}, f32[256]{0:T(256)S(1)}, f32[256]{0:T(256)}, /*index=5*/f32[16,256]{1,0:T(8,128)}, s32[]{:T(128)}) while((s32[]{:T(128)}, f32[257,256]{1,0:T(8,128)S(1)}, f32[16,256,256]{2,1,0:T(8,128)}, f32[256]{0:T(256)S(1)}, f32[256]{0:T(256)}, ...), condition=%wide.region_1.2_spmd.clone, body=%wide.region_0.1_spmd.clone.sunk | while | flops 202311168 | bytes 1322585 | solution.py:137
  8.7 1.4 fusion.109
  10.9 1.4 fusion.109
  13.1 1.4 fusion.109
  15.2 1.4 fusion.109
  17.4 1.4 fusion.109
  19.6 1.4 fusion.109
  21.7 1.4 fusion.109
  23.9 1.4 fusion.109
  26.1 1.4 fusion.109
  28.2 1.4 fusion.109
  30.4 1.4 fusion.109
  32.6 1.4 fusion.109
  34.7 1.4 fusion.109
  36.9 1.4 fusion.109
  39.1 1.4 fusion.109
  41.3 1.4 fusion.109
  42.6 1.5 stack.3
  44.2 5.2 %all-to-all-start = ((f32[4,1,257,256]{3,1,2,0:T(1,128)}), f32[4,1,257,256]{3,1,2,0:T(1,128)S(1)}, u32[]{:S(2)}, u32[]{:S(2)}) async-start(f32[4,1,257,256]{3,1,2,0:T(1,128)} %stack.3), calls=%async_computation | async-start | bytes 2105344 | tf_op jit(solution)/shard_map/all_to_all | solution.py:59
  49.4 13.6 %all-to-all-done = f32[4,1,257,256]{3,1,2,0:T(1,128)S(1)} async-done(((f32[4,1,257,256]{3,1,2,0:T(1,128)}), f32[4,1,257,256]{3,1,2,0:T(1,128)S(1)}, u32[]{:S(2)}, u32[]{:S(2)}) %all-to-all-start) | async-done | bytes 1052704 | tf_op jit(solution)/shard_map/all_to_all | solution.py:59
  63.2 7.5 %while.126 = (s32[]{:T(128)}, f32[257,256]{1,0:T(8,128)S(1)}, f32[257,256]{1,0:T(8,128)S(1)}, s32[4]{0:T(128)S(1)}, s32[]{:T(128)}, /*index=5*/f32[4,257,256]{2,1,0:T(8,128)S(1)}, s32[]{:T(128)}, s32[]{:T(128)}, s32[]{}) while((s32[]{:T(128)}, f32[257,256]{1,0:T(8,128)S(1)}, f32[257,256]{1,0:T(8,128)S(1)}, s32[4]{0:T(128)S(1)}, s32[]{:T(128)}, ...), condition=%wide.region_3.4_spmd, body=%wide.region_2.3_spmd.sunk | while | flops 202310912 | bytes 1861775 | solution.py:70
  74.6 27.0 %all-gather.8.cloned.1.call-done = f32[8,257,256]{2,1,0:T(8,128)} async-done(((f32[1,257,256]{2,1,0:T(8,128)}), f32[8,257,256]{2,1,0:T(8,128)}) %all-gather.8.cloned.1.call-update) | async-done | bytes 2105360 | tf_op jit(solution)/shard_map/all_gather | solution.py:11
  102.2 33.3 %while.128 = (s32[]{:T(128)}, f32[256]{0:T(256)S(1)}, f32[16,256]{1,0:T(8,128)S(1)}, f32[16,256]{1,0:T(8,128)S(1)}, f32[16,256,256]{2,1,0:T(8,128)}, /*index=5*/...) while((s32[]{:T(128)}, f32[256]{0:T(256)S(1)}, f32[16,256]{1,0:T(8,128)S(1)}, ...), condition=%wide.region_7.8_spmd, body=%wide.region_6.7_spmd.sunk | while | flops 787202 | bytes 275049 | solution.py:146
  108.5 1.2 fusion.99
  114.7 1.2 fusion.99
  123.1 1.2 fusion.99
  135.6 6.1 %while.132 = (s32[]{:T(128)}, f32[256]{0:T(256)S(1)}, f32[256,256]{1,0:T(8,128)S(1)}, f32[16,256]{1,0:T(8,128)S(1)}, s32[]{:T(128)}, /*index=5*/s32[]{:T(128)}, s32[]{:T(128)}) while((s32[]{:T(128)}, f32[256]{0:T(256)S(1)}, f32[256,256]{1,0:T(8,128)S(1)}, f32[16,256]{1,0:T(8,128)S(1)}, s32[]{:T(128)}, /*index=5*/s32[]{:T(128)}, ...), condition=%wide.region_9.10_spmd.clone, body=%wide.region_8.9_spmd.clone.sunk | while | flops 786948 | bytes 271463 | solution.py:154
  141.7 8.0 %all-gather.4 = f32[4,1,256]{2,1,0:T(1,128)S(1)} all-gather(f32[1,1,256]{2,1,0:T(1,128)S(1)} %bitcast.224), channel_id=3, replica_groups=mesh['inner'=4,'outer'=8] {'inner'}, dimensions={0}, use_global_device_ids=true | all-gather | bytes 5120 | tf_op jit(solution)/shard_map/all_gather | solution.py:87
  150.8 22.8 %all-gather.5 = f32[8,1,256]{2,1,0:T(1,128)S(1)} all-gather(f32[1,1,256]{2,1,0:T(1,128)S(1)} %bitcast.223), channel_id=4, replica_groups=mesh['inner'=4,'outer'=8] {'outer'}, dimensions={0}, use_global_device_ids=true | all-gather | bytes 9216 | tf_op jit(solution)/shard_map/all_gather | solution.py:107
  173.6 12.2 %while.134 = (s32[]{:T(128)}, f32[256]{0:T(256)S(1)}, f32[256]{0:T(256)S(1)}, f32[256,256]{1,0:T(8,128)S(1)}, f32[8,256]{1,0:T(8,128)S(1)}, /*index=5*/s32[8]{0:...) while((s32[]{:T(128)}, f32[256]{0:T(256)S(1)}, f32[256]{0:T(256)S(1)}, ...), condition=%wide.region_13.14_spmd.clone, body=%wide.region_12.13_spmd.clone.sunk | while | flops 787461 | bytes 273557 | solution.py:108
  185.8 6.0 %while.129 = (s32[]{:T(128)}, f32[256]{0:T(256)S(1)}, f32[256]{0:T(256)S(1)}, f32[256,256]{1,0:T(8,128)S(1)}, f32[4,256]{1,0:T(4,128)S(1)}, /*index=5*/s32[4]{0:T(128)S(1)}, s32[]{:T(128)}, s32[]{:T(128)}, s32[]{:T(128)}) while((s32[]{:T(128)}, f32[256]{0:T(256)S(1)}, f32[256]{0:T(256)S(1)}, f32[256,256]{1,0:T(8,128)S(1)}, ...), condition=%wide.region_15.16_spmd, body=%wide.region_14.15_spmd.sunk | while | flops 786948 | bytes 272515 | solution.py:114
  191.9 6.3 %while.130 = (s32[]{:T(128)}, f32[256]{0:T(256)S(1)}, f32[16,256]{1,0:T(8,128)S(1)}, f32[256,256]{1,0:T(8,128)S(1)}, f32[16,256]{1,0:T(8,128)S(1)}, /*index=5*/s32[]{:T(128)}, s32[]{:T(128)}, s32[]{:T(128)}) while((s32[]{:T(128)}, f32[256]{0:T(256)S(1)}, f32[16,256]{1,0:T(8,128)S(1)}, f32[256,256]{1,0:T(8,128)S(1)}, ...), condition=%wide.region_17.18_spmd, body=%wide.region_16.17_spmd.sunk | while | flops 786691 | bytes 271465 | solution.py:157
  (399 shorter events, 75.5 us)
Async XLA Ops:
  7.2 94.4 %copy-start = (f32[256]{0:T(256)S(1)}, f32[256]{0:T(256)}, u32[]{:S(2)}) copy-start(f32[256]{0:T(256)} %param.27) | copy-start | bytes 3076
  44.2 18.9 %all-to-all-start = ((f32[4,1,257,256]{3,1,2,0:T(1,128)}), f32[4,1,257,256]{3,1,2,0:T(1,128)S(1)}, u32[]{:S(2)}, u32[]{:S(2)}) async-start(f32[4,1,257,256]{3,1,2,0:T(1,128)} %stack.3), calls=%async_computation | async-start | bytes 2105344 | tf_op jit(solution)/shard_map/all_to_all | solution.py:59
  49.4 52.2 %all-gather.8.cloned.1.call-start = ((), (), s32[]{:S(2)}) async-start(), calls=%async_computation.1 | async-start | bytes 2433024 | tf_op jit(solution)/shard_map/all_gather | solution.py:11
  63.2 8.3 %copy-start.1 = (f32[256,256]{1,0:T(8,128)S(1)}, f32[256,256]{1,0:T(8,128)}, u32[]{:S(2)}) copy-start(f32[256,256]{1,0:T(8,128)} %param.26) | copy-start | bytes 786436
  70.7 0.7 copy-start.2
  101.6 0.7 copy-start.3
  135.6 38.1 %copy-start.4 = (f32[16,256]{1,0:T(8,128)}, f32[16,256]{1,0:T(8,128)S(1)}, u32[]{:S(2)}) copy-start(f32[16,256]{1,0:T(8,128)S(1)} %get-tuple-element.684) | copy-start | bytes 49156
Sparse Core Ops, SparseCore 0:
  71.5 30.0 all-gather.7
